TPU v7x, 512 devices: a whole 4x4x16 slice. The times are simulated.
512 devices in a mesh: space: 32 (over z_lo, x, core), species: 16 (over y, z_hi).
Axes of the slice: x: 4, y: 4, z: 16 (z_hi: 4, z_lo: 4; z = z_hi * 4 + z_lo), core: 2. Of those that a mesh axis runs over, the one named last changes fastest.
Arguments:
- biomass: bfloat16 [512, 64, 1024], P('species', 'space'), may hold values from 0.019897461 to 1
- resources: float32 [128, 64, 1024], P('species', 'space'), may hold values from 0.1 to 4
- capacity: float32 [512, 128], P('species'), may hold values from 0.002 to 0.05
- affinity: float32 [512, 128], P('species'), may hold values from 0.2 to 5
- secretion: bfloat16 [128, 512], P(None, 'species'), may hold values from 0 to 0.059814453
- energy_yield: float32 [128], replicated, may hold values from 0.5 to 2
- maintenance: float32 [512], P('species'), may hold values from 0.3 to 3
- motility: float32 [512], P('species'), may hold values from 0.04 to 0.6
- diffusivity: float32 [128], P('species'), may hold values from 0.02 to 0.6
- supply: float32 [128], P('species'), may hold values from 0.4 to 4
Outputs:
- growth: float32 [512, 64, 1024], P('species', 'space')
- new_biomass: float32 [512, 64, 1024], P('species', 'space')
- new_resources: float32 [128, 64, 1024], P('species', 'space')
All inputs are finite; a program needn't handle non-finite values.
Results may differ from a plain program's by a relative error of at most 0.0003.
Values may be sent and summed in bfloat16 or wider, within the bound.
A program may use at most 64 MiB of HBM per device.

v0:
```python
import math
import jax
import jax.numpy as jnp
from jax import lax
from jax.sharding import PartitionSpec as P

NY = 16
NZ = 64
time_step = 0.25


def extended_2(block, sides, width):
    for axis, dim in sides:
        count = lax.axis_size(axis)
        forward = [(i, i + 1) for i in range(count - 1)]
        forward.append((count - 1, 0))
        backward = [(target, source) for source, target in forward]
        low = lax.ppermute(
            lax.slice_in_dim(block, block.shape[dim] - width, None, axis=dim), axis, forward
        )
        high = lax.ppermute(lax.slice_in_dim(block, 0, width, axis=dim), axis, backward)
        block = jnp.concatenate([low, block, high], axis=dim)
    return block


def laplace(padded, depth_cells, width_cells):
    channel_count = padded.shape[0]
    inner_cells = padded[:, 1:-1, :]
    slab_rows = inner_cells.shape[1]
    block_view = inner_cells.reshape(channel_count, slab_rows, depth_cells, width_cells)
    extended = jnp.pad(block_view, ((0, 0), (0, 0), (1, 1), (1, 1)), mode="edge")
    beside_x = padded[:, 2:, :] + padded[:, :-2, :]
    beside_yz = (
        extended[:, :, 2:, 1:-1]
        + extended[:, :, :-2, 1:-1]
        + extended[:, :, 1:-1, 2:]
        + extended[:, :, 1:-1, :-2]
    )
    return beside_x + beside_yz.reshape(channel_count, slab_rows, -1) - 6.0 * inner_cells


def spread_biomass(biomass, motility):
    padded = extended_2(biomass, (("space", 1),), 1).astype(jnp.float32)
    return motility[:, None, None] * laplace(padded, NY, NZ)


def spread_resources(resources, diffusivity):
    padded = extended_2(resources, (("space", 1),), 1)
    return diffusivity[:, None, None] * laplace(padded, NY, NZ)


def per_device(
    biomass,
    resources,
    capacity,
    affinity,
    secretion,
    energy_yield,
    maintenance,
    motility,
    diffusivity,
    supply,
):
    local_strains, slab_rows, plane_cells = biomass.shape
    cells_dev = slab_rows * plane_cells
    seen = lax.all_gather(resources.astype(jnp.bfloat16), "species", axis=0, tiled=True)
    all_resources = seen.shape[0]
    seen_flat = seen.reshape(all_resources, cells_dev)
    mass_flat = biomass.reshape(local_strains, cells_dev)
    block_cells = math.gcd(256, cells_dev)
    block_count = cells_dev // block_cells

    def per_block(block_index, carry):
        growth_all, consumed_all, secreted_all = carry
        start = block_index * block_cells
        seen_block = lax.dynamic_slice_in_dim(seen_flat, start, block_cells, 1).astype(jnp.float32)
        mass_block = lax.dynamic_slice_in_dim(mass_flat, start, block_cells, 1).astype(jnp.float32)
        uptake = (
            capacity[:, :, None]
            * seen_block[None, :, :]
            / (affinity[:, :, None] + seen_block[None, :, :])
        )
        growth_block = jnp.sum(energy_yield[None, :, None] * uptake, axis=1) - maintenance[:, None]
        flux_block = jnp.sum(uptake, axis=1)
        product_block = (mass_block * flux_block).astype(jnp.bfloat16)
        consumed_block = jnp.sum(mass_block[:, None, :] * uptake, axis=0)
        secreted_block = jnp.dot(secretion, product_block, preferred_element_type=jnp.float32)
        growth_all = lax.dynamic_update_slice_in_dim(growth_all, growth_block, start, 1)
        consumed_all = lax.dynamic_update_slice_in_dim(consumed_all, consumed_block, start, 1)
        secreted_all = lax.dynamic_update_slice_in_dim(secreted_all, secreted_block, start, 1)
        return (growth_all, consumed_all, secreted_all)

    initial = (
        jnp.zeros((local_strains, cells_dev), jnp.float32),
        jnp.zeros((all_resources, cells_dev), jnp.float32),
        jnp.zeros((all_resources, cells_dev), jnp.float32),
    )
    growth_all, consumed_all, secreted_all = lax.fori_loop(0, block_count, per_block, initial)
    growth = growth_all.reshape(local_strains, slab_rows, plane_cells)
    consumed_all = consumed_all.reshape(all_resources, slab_rows, plane_cells)
    secreted_all = secreted_all.reshape(all_resources, slab_rows, plane_cells)
    consumed_owned, secreted_owned = (
        lax.psum_scatter(consumed_all, "species", scatter_dimension=0, tiled=True),
        lax.psum_scatter(secreted_all, "species", scatter_dimension=0, tiled=True),
    )
    net_owned = secreted_owned - consumed_owned
    mass_spread = spread_biomass(biomass, motility)
    resource_spread = spread_resources(resources, diffusivity)
    mass = biomass.astype(jnp.float32)
    new_biomass = mass + time_step * (mass * growth + mass_spread)
    new_resources = resources + time_step * (resource_spread + net_owned + supply[:, None, None])
    return (growth, new_biomass, new_resources)


def solution(mesh):
    return jax.shard_map(
        per_device,
        mesh=mesh,
        in_specs=(
            P("species", "space", None),
            P("species", "space", None),
            P("species", None),
            P("species", None),
            P(None, "species"),
            P(),
            P("species"),
            P("species"),
            P("species"),
            P("species"),
        ),
        out_specs=(
            P("species", "space", None),
            P("species", "space", None),
            P("species", "space", None),
        ),
        check_vma=False,
    )
```

profile of v0, /device:TPU:78, one launch (start us, length us, event | category | flops | bytes accessed | tf_op | source)
XLA Modules:
  0.0 375.8 jit_solution(9521856368249420357)
XLA Ops:
  7.2 0.0 all-reduce.5.cloned.1.call-start
  7.2 0.9 convert_element_type.30
  8.1 57.8 %all_gather.3 = bf16[128,2,1024]{2,1,0:T(2,128)(2,1)S(1)} all-gather(bf16[8,2,1024]{2,1,0:T(2,128)(2,1)S(1)} %convert_element_type.30), channel_id=1, replica_groups=mesh['space'=32,'species'=16] {'species'}, dimensions={0}, use_global_device_ids=true | all-gather | bytes 557056 | tf_op jit(solution)/shard_map/all_gather | solution.py:66
  65.9 0.1 copy.20
  66.1 0.0 copy-start.3
  66.1 0.0 copy-start.4
  66.1 0.0 copy-start.5
  66.2 0.0 copy-start.7
  66.2 0.1 broadcast.12
  66.3 0.1 broadcast.12.clone
  66.4 0.5 copy-done.3
  66.8 0.0 copy-done.4
  66.9 20.4 %while.17 = (s32[]{:T(128)}, f32[32,2048]{1,0:T(8,128)S(1)}, f32[128,2048]{1,0:T(8,128)S(1)}, f32[128,2048]{0,1:T(8,128)S(1)}, f32[128]{0:T(128)S(1)}, /*index=5...) while((s32[]{:T(128)}, f32[32,2048]{1,0:T(8,128)S(1)}, ...), condition=%wide.region_4.0_spmd, body=%wide.region_0.0_spmd.sunk | while | flops 10510342 | bytes 1157331 | solution.py:98
  66.9 2.2 fusion.32
  69.1 0.1 subtract_dynamic-update-slice_fusion.2
  69.2 0.2 fusion.33
  69.5 2.2 fusion.32
  71.7 0.1 subtract_dynamic-update-slice_fusion.2
  71.8 0.2 fusion.33
  72.0 2.2 fusion.32
  74.2 0.1 subtract_dynamic-update-slice_fusion.2
  74.3 0.2 fusion.33
  74.6 2.2 fusion.32
  76.8 0.1 subtract_dynamic-update-slice_fusion.2
  76.9 0.2 fusion.33
  77.1 2.2 fusion.32
  79.3 0.1 subtract_dynamic-update-slice_fusion.2
  79.4 0.2 fusion.33
  79.7 2.2 fusion.32
  81.9 0.1 subtract_dynamic-update-slice_fusion.2
  82.0 0.2 fusion.33
  82.2 2.2 fusion.32
  84.4 0.1 subtract_dynamic-update-slice_fusion.2
  84.5 0.2 fusion.33
  84.8 2.2 fusion.32
  87.0 0.1 subtract_dynamic-update-slice_fusion.2
  87.1 0.2 fusion.33
  87.3 1.9 reshape.50
  89.1 1.3 copy.19
  90.5 0.0 all-reduce.5.cloned.1.call-update
  90.5 0.2 fusion.25
  90.7 1.9 collective-permute-start.1
  92.6 2.4 collective-permute-start
  95.0 0.1 fusion.26
  95.1 1.9 collective-permute-start.3
  97.0 3.6 collective-permute-start.2
  100.7 0.1 reshape.47
  100.8 0.2 reshape.44
  101.0 0.0 copy-start.1
  101.1 0.1 fusion.23
  101.2 0.2 fusion.11
  101.5 0.1 reshape.48
  101.6 1.3 dynamic-slice
  103.5 0.4 maximum_convert_fusion
  103.9 0.1 slice.124
  104.1 0.3 reshape.45
  104.5 0.1 pad_maximum_fusion
  104.6 0.3 fusion.21
  104.9 0.7 fusion.3
  105.6 0.3 reshape.46
  105.9 0.0 copy-start.10
  105.9 1.2 convert_add_fusion
  107.1 260.1 %all-reduce.5.cloned.1.call-done = (f32[128,2,1024]{2,1,0:T(2,128)}, f32[128,2,1024]{2,1,0:T(2,128)}) async-done(((f32[128,2,1024]{2,1,0:T(2,128)}, f32[128,2,1024]{2,1,0:T(2,128)}), (f32[128,2,1024]{2,1,0:T(2,128)}, f32[128,2,1024]{2,1,0:T(2,128)})) %all-reduce.5.cloned.1.call-update) | async-done | bytes 2097168
  367.2 1.7 fusion.20
  (47 shorter events, 0.5 us)
Async XLA Ops:
  7.2 58.9 %copy-start = (bf16[32,2,1024]{2,1,0:T(2,128)(2,1)S(1)}, bf16[32,2,1024]{2,1,0:T(2,128)(2,1)}, u32[]{:S(2)}) copy-start(bf16[32,2,1024]{2,1,0:T(2,128)(2,1)} %param.12) | copy-start | bytes 393220
  7.2 360.0 %all-reduce.5.cloned.1.call-start = ((), (), s32[]{:S(2)}) async-start(), calls=%async_computation | async-start | bytes 4194304
  66.1 0.7 copy-start.3
  66.1 0.7 copy-start.4
  66.1 0.7 copy-start.5
  66.1 0.7 copy-start.6
  66.2 0.7 copy-start.7
  90.5 4.6 %copy-start.2 = (f32[8,2,1024]{2,1,0:T(2,128)S(1)}, f32[8,2,1024]{2,1,0:T(2,128)}, u32[]{:S(2)}) copy-start(f32[8,2,1024]{2,1,0:T(2,128)} %param.13) | copy-start | bytes 196612
  90.7 12.8 %collective-permute-start.1 = (bf16[32,1,1024]{2,1,0:T(2,128)(2,1)S(1)}, bf16[32,1,1024]{2,1,0:T(2,128)(2,1)S(1)}, u32[]{:S(2)}, u32[]{:S(2)}) collective-permute-start(bf16[32,1,1024]{2,1,0:T(2,128)(2,1)S(1)} %get-tuple-element.261), channel_id=1, source_target_pairs={{16,0},{32,16},{48,32},{64,48},{80,64},{96,80},{112,96},{128,112},... | collective-permute-start | bytes 196616 | tf_op jit(solution)/shard_map/ppermute | solution.py:21
  92.6 10.9 %collective-permute-start = (bf16[32,1,1024]{2,1,0:T(2,128)(2,1)S(1)}, bf16[32,1,1024]{2,1,0:T(2,128)(2,1)S(1)}, u32[]{:S(2)}, u32[]{:S(2)}) collective-permute-start(bf16[32,1,1024]{2,1,0:T(2,128)(2,1)S(1)} %get-tuple-element.260), channel_id=1, source_target_pairs={{0,16},{16,32},{32,48},{48,64},{64,80},{80,96},{96,112},{112,128},... | collective-permute-start | bytes 196616 | tf_op jit(solution)/shard_map/ppermute | solution.py:18
  95.1 12.0 %collective-permute-start.3 = (f32[8,1,1024]{2,1,0:T(1,128)S(1)}, f32[8,1,1024]{2,1,0:T(1,128)S(1)}, u32[]{:S(2)}, u32[]{:S(2)}) collective-permute-start(f32[8,1,1024]{2,1,0:T(1,128)S(1)} %get-tuple-element.263), channel_id=1, source_target_pairs={{0,16},{16,32},{32,48},{48,64},{64,80},{80,96},{96,112},{112,128},... | collective-permute-start | bytes 98312 | tf_op jit(solution)/shard_map/ppermute | solution.py:18
  97.0 10.1 %collective-permute-start.2 = (f32[8,1,1024]{2,1,0:T(1,128)S(1)}, f32[8,1,1024]{2,1,0:T(1,128)S(1)}, u32[]{:S(2)}, u32[]{:S(2)}) collective-permute-start(f32[8,1,1024]{2,1,0:T(1,128)S(1)} %get-tuple-element.262), channel_id=1, source_target_pairs={{16,0},{32,16},{48,32},{64,48},{80,64},{96,80},{112,96},{128,112},... | collective-permute-start | bytes 98312 | tf_op jit(solution)/shard_map/ppermute | solution.py:21
  101.0 4.8 %copy-start.1 = (f32[32,2,1024]{2,1,0:T(2,128)}, f32[32,2,1024]{2,1,0:T(2,128)S(1)}, u32[]{:S(2)}) copy-start(f32[32,2,1024]{2,1,0:T(2,128)S(1)} %reshape.44) | copy-start | bytes 786436
  104.9 0.9 copy-start.8
  105.8 261.4 %copy-start.9 = (f32[8]{0:T(128)S(1)}, f32[8]{0:T(128)}, u32[]{:S(2)}) copy-start(f32[8]{0:T(128)} %param.21) | copy-start | bytes 100
  105.9 261.4 %copy-start.10 = (f32[8]{0:T(128)S(1)}, f32[8]{0:T(128)}, u32[]{:S(2)}) copy-start(f32[8]{0:T(128)} %param.20) | copy-start | bytes 100
Sparse Core Ops, SparseCore 0:
  90.6 276.5 all-reduce.4
where the time goes:
time: 376 us
  waiting for transfers between devices  260 us (69%)
  blocking collectives  57.8 us (15%)
  other arithmetic  23.6 us (6%)
  between operations  15 us (4%)
  starting transfers between devices  9.93 us (3%)
  local copies, waits for them, and re-layouts  7.3 us (2%)
    unnamed x2, waiting for transfers between devices  260 us
    all_gather x1, blocking collectives, per_device(): lax.all_gather(resources.astype(jnp.bfloat16), 'species', axis=0, tiled=T...  57.8 us
    reduce_sum x8, other arithmetic, per_block(): flux_block = jnp.sum(uptake, axis=1)  17.5 us
  transfers between devices with their start and end apart: 5, of which 1 were waited for; matrix products, arithmetic and copies ran while one was open for 2% of the time, Pallas kernels for 0%

commit v1 on v0

--- a/solution.py
+++ b/solution.py
@@ -63,7 +63,12 @@
 ):
     local_strains, slab_rows, plane_cells = biomass.shape
     cells_dev = slab_rows * plane_cells
-    seen = lax.all_gather(resources.astype(jnp.bfloat16), "species", axis=0, tiled=True)
+    seen = jnp.concatenate(
+        lax.all_to_all(
+            jnp.stack([resources.astype(jnp.bfloat16)] * lax.axis_size("species")), "species", 0, 0
+        ),
+        axis=0,
+    )
     all_resources = seen.shape[0]
     seen_flat = seen.reshape(all_resources, cells_dev)
     mass_flat = biomass.reshape(local_strains, cells_dev)

time: 376 us -> 360 us (0.957)
  blocking collectives: 57.8 us -> 0 us
  waiting for transfers between devices: 260 us -> 284 us
  starting transfers between devices: 9.93 us -> 26.3 us
    all_gather x1 -> x0, blocking collectives: 57.8 us -> none  [per_device(): lax.all_gather(resources.astype(jnp.bfloat16), 'species', axis=0, tiled=T...]
    all_to_all x0 -> x1, waiting for transfers between devices: none -> 32.6 us  [per_device(): lax.all_to_all(jnp.stack([resources.astype(jnp.bfloat16)] * lax.axis_size...]
    all_to_all x0 -> x1, starting transfers between devices: none -> 16.4 us  [per_device(): lax.all_to_all(jnp.stack([resources.astype(jnp.bfloat16)] * lax.axis_size...]
    unnamed x2, waiting for transfers between devices: 260 us -> 251 us
  transfers between devices with their start and end apart: 5 -> 6, of which waited for: 1 -> 2; matrix products, arithmetic and copies ran while one was open for 2% -> 2% of each run, Pallas kernels for 0% -> 0%
where the time goes in v1:
time: 360 us; the launch traced here: 359 us
  waiting for transfers between devices  284 us (79%)
  starting transfers between devices  26.3 us (7%)
  other arithmetic  23.6 us (7%)
  between operations  15 us (4%)
  local copies, waits for them, and re-layouts  8.18 us (2%)
    unnamed x2, waiting for transfers between devices  251 us
    all_to_all x1, waiting for transfers between devices, per_device(): lax.all_to_all(jnp.stack([resources.astype(jnp.bfloat16)] * lax.axis_size...  32.6 us
    reduce_sum x8, other arithmetic, per_block(): flux_block = jnp.sum(uptake, axis=1)  17.5 us
    all_to_all x1, starting transfers between devices, per_device(): lax.all_to_all(jnp.stack([resources.astype(jnp.bfloat16)] * lax.axis_size...  16.4 us
  transfers between devices with their start and end apart: 6, of which 2 were waited for; matrix products, arithmetic and copies ran while one was open for 2% of the time, Pallas kernels for 0%

profile of v1, /device:TPU:78, one launch (start us, length us, event | category | flops | bytes accessed | tf_op | source)
XLA Modules:
  0.0 359.1 jit_solution(3247437523294100946)
XLA Ops:
  7.2 0.9 convert_element_type.30
  8.1 0.9 stack.2
  9.0 16.4 %all-to-all-start = ((bf16[16,8,2,1024]{3,1,2,0:T(8,128)(2,1)}), bf16[16,8,2,1024]{3,1,2,0:T(8,128)(2,1)S(1)}, u32[]{:S(2)}, u32[]{:S(2)}) async-start(bf16[16,8,2,1024]{3,1,2,0:T(8,128)(2,1)} %stack.2), calls=%async_computation | async-start | bytes 1048576 | tf_op jit(solution)/shard_map/all_to_all | solution.py:67
  25.3 0.0 all-reduce.5.cloned.1.call-start
  25.4 32.6 %all-to-all-done = bf16[16,8,2,1024]{3,1,2,0:T(8,128)(2,1)S(1)} async-done(((bf16[16,8,2,1024]{3,1,2,0:T(8,128)(2,1)}), bf16[16,8,2,1024]{3,1,2,0:T(8,128)(2,1)S(1)}, u32[]{:S(2)}, u32[]{:S(2)}) %all-to-all-start) | async-done | bytes 524320 | tf_op jit(solution)/shard_map/all_to_all | solution.py:67
  58.1 0.0 copy-start.3
  58.1 0.0 copy-start.6
  58.1 0.0 copy-start.7
  58.1 0.1 broadcast.14
  58.2 0.1 broadcast.14.clone
  58.3 0.5 copy-done.3
  58.8 0.0 copy-done.4
  58.8 20.4 %while.17 = (s32[]{:T(128)}, f32[32,2048]{1,0:T(8,128)S(1)}, f32[128,2048]{1,0:T(8,128)S(1)}, f32[128,2048]{0,1:T(8,128)S(1)}, f32[128]{0:T(128)S(1)}, /*index=5...) while((s32[]{:T(128)}, f32[32,2048]{1,0:T(8,128)S(1)}, ...), condition=%wide.region_4.0_spmd, body=%wide.region_0.0_spmd.sunk | while | flops 10510342 | bytes 1157331 | solution.py:103
  58.9 2.2 fusion.32
  61.1 0.1 subtract_dynamic-update-slice_fusion.2
  61.2 0.2 fusion.33
  61.4 2.2 fusion.32
  63.6 0.1 subtract_dynamic-update-slice_fusion.2
  63.7 0.2 fusion.33
  64.0 2.2 fusion.32
  66.2 0.1 subtract_dynamic-update-slice_fusion.2
  66.3 0.2 fusion.33
  66.5 2.2 fusion.32
  68.7 0.1 subtract_dynamic-update-slice_fusion.2
  68.8 0.2 fusion.33
  69.1 2.2 fusion.32
  71.3 0.1 subtract_dynamic-update-slice_fusion.2
  71.4 0.2 fusion.33
  71.6 2.2 fusion.32
  73.8 0.1 subtract_dynamic-update-slice_fusion.2
  73.9 0.2 fusion.33
  74.2 2.2 fusion.32
  76.4 0.1 subtract_dynamic-update-slice_fusion.2
  76.5 0.2 fusion.33
  76.8 2.2 fusion.32
  79.0 0.1 subtract_dynamic-update-slice_fusion.2
  79.0 0.2 fusion.33
  79.2 1.9 reshape.48
  81.1 1.3 copy.22
  82.4 0.0 all-reduce.5.cloned.1.call-update
  82.5 0.2 fusion.25
  82.6 1.9 collective-permute-start.1
  84.6 2.4 collective-permute-start
  87.0 0.1 fusion.26
  87.1 3.1 collective-permute-start.3
  90.2 2.5 collective-permute-start.2
  92.6 0.1 reshape.45
  92.8 0.1 fusion.23
  93.0 0.2 fusion.11
  93.2 0.1 reshape.46
  93.3 1.3 dynamic-slice
  95.2 0.4 maximum_convert_fusion
  95.7 0.1 slice.124
  95.8 0.3 reshape.43
  96.2 0.1 pad_maximum_fusion
  96.3 0.3 fusion.21
  96.6 0.7 fusion.3
  97.3 0.3 reshape.44
  97.6 0.0 copy-start.9
  97.6 0.2 reshape.42
  97.8 0.1 copy-done.8
  97.9 1.2 convert_add_fusion
  99.1 251.4 %all-reduce.5.cloned.1.call-done = (f32[128,2,1024]{2,1,0:T(2,128)}, f32[128,2,1024]{2,1,0:T(2,128)}) async-done(((f32[128,2,1024]{2,1,0:T(2,128)}, f32[128,2,1024]{2,1,0:T(2,128)}), (f32[128,2,1024]{2,1,0:T(2,128)}, f32[128,2,1024]{2,1,0:T(2,128)})) %all-reduce.5.cloned.1.call-update) | async-done | bytes 2097168
  350.6 1.7 fusion.20
  (49 shorter events, 0.5 us)
Async XLA Ops:
  7.2 18.2 %copy-start = (bf16[32,2,1024]{2,1,0:T(2,128)(2,1)S(1)}, bf16[32,2,1024]{2,1,0:T(2,128)(2,1)}, u32[]{:S(2)}) copy-start(bf16[32,2,1024]{2,1,0:T(2,128)(2,1)} %param.12) | copy-start | bytes 393220
  9.0 49.1 %all-to-all-start = ((bf16[16,8,2,1024]{3,1,2,0:T(8,128)(2,1)}), bf16[16,8,2,1024]{3,1,2,0:T(8,128)(2,1)S(1)}, u32[]{:S(2)}, u32[]{:S(2)}) async-start(bf16[16,8,2,1024]{3,1,2,0:T(8,128)(2,1)} %stack.2), calls=%async_computation | async-start | bytes 1048576 | tf_op jit(solution)/shard_map/all_to_all | solution.py:67
  25.3 325.2 %all-reduce.5.cloned.1.call-start = ((), (), s32[]{:S(2)}) async-start(), calls=%async_computation.1 | async-start | bytes 4194304
  58.1 0.7 copy-start.3
  58.1 0.7 copy-start.4
  58.1 0.7 copy-start.5
  58.1 0.7 copy-start.6
  58.1 0.7 copy-start.7
  82.4 4.6 %copy-start.2 = (f32[8,2,1024]{2,1,0:T(2,128)S(1)}, f32[8,2,1024]{2,1,0:T(2,128)}, u32[]{:S(2)}) copy-start(f32[8,2,1024]{2,1,0:T(2,128)} %param.13) | copy-start | bytes 196612
  82.6 12.6 %collective-permute-start.1 = (bf16[32,1,1024]{2,1,0:T(2,128)(2,1)S(1)}, bf16[32,1,1024]{2,1,0:T(2,128)(2,1)S(1)}, u32[]{:S(2)}, u32[]{:S(2)}) collective-permute-start(bf16[32,1,1024]{2,1,0:T(2,128)(2,1)S(1)} %get-tuple-element.261), channel_id=1, source_target_pairs={{16,0},{32,16},{48,32},{64,48},{80,64},{96,80},{112,96},{128,112},... | collective-permute-start | bytes 196616 | tf_op jit(solution)/shard_map/ppermute | solution.py:21
  84.6 10.7 %collective-permute-start = (bf16[32,1,1024]{2,1,0:T(2,128)(2,1)S(1)}, bf16[32,1,1024]{2,1,0:T(2,128)(2,1)S(1)}, u32[]{:S(2)}, u32[]{:S(2)}) collective-permute-start(bf16[32,1,1024]{2,1,0:T(2,128)(2,1)S(1)} %get-tuple-element.260), channel_id=1, source_target_pairs={{0,16},{16,32},{32,48},{48,64},{64,80},{80,96},{96,112},{112,128},... | collective-permute-start | bytes 196616 | tf_op jit(solution)/shard_map/ppermute | solution.py:18
  87.1 12.1 %collective-permute-start.3 = (f32[8,1,1024]{2,1,0:T(1,128)S(1)}, f32[8,1,1024]{2,1,0:T(1,128)S(1)}, u32[]{:S(2)}, u32[]{:S(2)}) collective-permute-start(f32[8,1,1024]{2,1,0:T(1,128)S(1)} %get-tuple-element.263), channel_id=1, source_target_pairs={{0,16},{16,32},{32,48},{48,64},{64,80},{80,96},{96,112},{112,128},... | collective-permute-start | bytes 98312 | tf_op jit(solution)/shard_map/ppermute | solution.py:18
  90.2 9.0 %collective-permute-start.2 = (f32[8,1,1024]{2,1,0:T(1,128)S(1)}, f32[8,1,1024]{2,1,0:T(1,128)S(1)}, u32[]{:S(2)}, u32[]{:S(2)}) collective-permute-start(f32[8,1,1024]{2,1,0:T(1,128)S(1)} %get-tuple-element.262), channel_id=1, source_target_pairs={{16,0},{32,16},{48,32},{64,48},{80,64},{96,80},{112,96},{128,112},... | collective-permute-start | bytes 98312 | tf_op jit(solution)/shard_map/ppermute | solution.py:21
  97.3 0.7 copy-start.8
  97.6 253.0 %copy-start.9 = (f32[8]{0:T(128)S(1)}, f32[8]{0:T(128)}, u32[]{:S(2)}) copy-start(f32[8]{0:T(128)} %param.21) | copy-start | bytes 100
  97.6 253.0 %copy-start.10 = (f32[8]{0:T(128)S(1)}, f32[8]{0:T(128)}, u32[]{:S(2)}) copy-start(f32[8]{0:T(128)} %param.20) | copy-start | bytes 100
  97.9 254.4 %copy-start.1 = (f32[32,2,1024]{2,1,0:T(2,128)}, f32[32,2,1024]{2,1,0:T(2,128)S(1)}, u32[]{:S(2)}) copy-start(f32[32,2,1024]{2,1,0:T(2,128)S(1)} %reshape.42) | copy-start | bytes 786436
Sparse Core Ops, SparseCore 0:
  82.6 267.9 all-reduce.4
